TPU v7x, 32 devices: a whole 2x2x4 slice. The times are simulated.
32 devices in a mesh: gx: 4 (over x, core), yz: 8 (over z, y).
Axes of the slice: x: 2, y: 2, z: 4, core: 2. Of those that a mesh axis runs over, the one named last changes fastest.
Arguments:
- stream: bfloat16 [128, 9216], P('yz', 'gx'), may hold values from -1700 to 1700
- ln_gain: bfloat16 [9216], P('gx'), may hold values from 0.099609375 to 1.8984375
- q_weight: bfloat16 [9216, 12288], P('gx', 'yz'), may hold values from -0.0625 to 0.0625
- kv_weight: bfloat16 [9216, 512], P('gx', 'yz'), may hold values from -0.0625 to 0.0625
- out_weight: bfloat16 [12288, 9216], P('yz', 'gx'), may hold values from -0.0546875 to 0.0546875
- gate_weight: bfloat16 [9216, 36864], P('gx', 'yz'), may hold values from -0.0625 to 0.0625
- up_weight: bfloat16 [9216, 36864], P('gx', 'yz'), may hold values from -0.0625 to 0.0625
- down_weight: bfloat16 [36864, 9216], P('yz', 'gx'), may hold values from -0.03125 to 0.03125
- cache: bfloat16 [128, 1536, 512], P(('gx', 'yz')), may hold values from -620 to 620
- lengths: int32 [128], P(('gx', 'yz')), may hold values from 1 to 1536, as said below
Outputs:
- update: bfloat16 [128, 9216], P('yz', 'gx')
Inputs may be any that keep to these rules, and one draw needn't show every extreme that they name: `lengths`: in every draw some sequence has all 1536 slots filled.
All inputs are finite; a program needn't handle non-finite values.
Results may differ from a plain program's by a relative error of at most 0.0082.
Values may be sent and summed in bfloat16 or wider, within the bound.
A program may use at most 192 MiB of HBM per device.

v0:
```python
import math

import jax
import jax.numpy as jnp
from jax import lax
from jax.sharding import PartitionSpec as P

D = 9216


def attend_local(query, new_kv, cache, lengths):
    seqs = query.shape[0]
    head_dim = cache.shape[2] // 2
    heads = query.shape[1] // head_dim
    query_vectors = query.reshape(seqs, heads, head_dim)
    key_rows = cache[:, :, :head_dim]
    value_rows = cache[:, :, head_dim:]
    new_key = new_kv[:, :head_dim]
    new_value = new_kv[:, head_dim:]
    score_scale = 1.0 / math.sqrt(head_dim)
    attention_logits = (
        jnp.einsum("tgb,twb->tgw", query_vectors, key_rows, preferred_element_type=jnp.float32)
        * score_scale
    )
    own = (
        jnp.einsum("shd,sd->sh", query_vectors, new_key, preferred_element_type=jnp.float32)
        * score_scale
    )
    positions = lax.broadcasted_iota(jnp.int32, (1, 1, cache.shape[1]), 2)
    valid = positions < lengths[:, None, None]
    top = jnp.maximum(jnp.max(jnp.where(valid, attention_logits, own[:, :, None]), axis=2), own)
    weights = jnp.where(valid, jnp.exp(attention_logits - top[:, :, None]), jnp.float32(0.0))
    own_weight = jnp.exp(own - top)
    denom = jnp.sum(weights, axis=2) + own_weight
    attention_probabilities = (weights / denom[:, :, None]).astype(jnp.bfloat16)
    own_prob = (own_weight / denom).astype(jnp.bfloat16)
    value_mixture = jnp.einsum(
        "aqc,acn->aqn", attention_probabilities, value_rows, preferred_element_type=jnp.float32
    )
    value_mixture = (
        value_mixture
        + own_prob.astype(jnp.float32)[:, :, None] * new_value.astype(jnp.float32)[:, None, :]
    )
    return value_mixture.astype(jnp.bfloat16).reshape(seqs, heads * head_dim)


def body(
    stream,
    ln_gain,
    q_weight,
    kv_weight,
    out_weight,
    gate_weight,
    up_weight,
    down_weight,
    cache,
    lengths,
):
    values_f = stream.astype(jnp.float32)
    total, squares = lax.psum(
        (jnp.sum(values_f, axis=1), jnp.sum(values_f * values_f, axis=1)), "gx"
    )
    mean = total / D
    variance = squares / D - mean * mean
    normed = (
        (values_f - mean[:, None])
        * lax.rsqrt(variance + 1e-05)[:, None]
        * ln_gain.astype(jnp.float32)[None, :]
    ).astype(jnp.bfloat16)
    gathered = lax.all_gather(normed, "yz", axis=0, tiled=True)
    query_part = jnp.dot(gathered, q_weight, preferred_element_type=jnp.float32)
    kv_part = jnp.dot(gathered, kv_weight, preferred_element_type=jnp.float32)
    query_block, kv_block = (
        lax.psum_scatter(query_part, "gx", scatter_dimension=0, tiled=True),
        lax.psum_scatter(kv_part, "gx", scatter_dimension=0, tiled=True),
    )
    query_own, kv_own = (
        lax.all_to_all(
            query_block.astype(jnp.bfloat16), "yz", split_axis=0, concat_axis=1, tiled=True
        ),
        lax.all_to_all(
            kv_block.astype(jnp.bfloat16), "yz", split_axis=0, concat_axis=1, tiled=True
        ),
    )
    attended = attend_local(query_own, kv_own, cache, lengths)
    head_block = lax.all_to_all(attended, "yz", split_axis=1, concat_axis=0, tiled=True)
    head_all = lax.all_gather(head_block, "gx", axis=0, tiled=True)
    gate_part = jnp.dot(gathered, gate_weight, preferred_element_type=jnp.float32)
    up_part = jnp.dot(gathered, up_weight, preferred_element_type=jnp.float32)
    gate_share, up_share = (
        lax.psum_scatter(gate_part, "gx", scatter_dimension=0, tiled=True),
        lax.psum_scatter(up_part, "gx", scatter_dimension=0, tiled=True),
    )
    hidden_share = (jax.nn.silu(gate_share) * up_share).astype(jnp.bfloat16)
    hidden = lax.all_gather(hidden_share, "gx", axis=0, tiled=True)
    first = jnp.dot(head_all, out_weight, preferred_element_type=jnp.float32)
    update = lax.psum_scatter(
        first + jnp.dot(hidden, down_weight, preferred_element_type=jnp.float32),
        "yz",
        scatter_dimension=0,
        tiled=True,
    )
    return update.astype(jnp.bfloat16)


def solution(mesh):
    return jax.shard_map(
        body,
        mesh=mesh,
        in_specs=(
            P("yz", "gx"),
            P("gx"),
            P("gx", "yz"),
            P("gx", "yz"),
            P("yz", "gx"),
            P("gx", "yz"),
            P("gx", "yz"),
            P("yz", "gx"),
            P(("gx", "yz"), None, None),
            P(("gx", "yz")),
        ),
        out_specs=P("yz", "gx"),
        check_vma=False,
    )
```

profile of v0, /device:TPU:0, one launch (start us, length us, event | category | flops | bytes accessed | tf_op | source)
XLA Modules:
  0.0 278.6 jit_solution(908472190213945265)
XLA Ops:
  6.5 0.0 copy-start
  6.5 0.0 reduce-scatter.8.cloned.1.call-start
  6.5 1.1 convert_reduce_fusion
  7.6 0.7 convert_element_type.37
  8.3 8.3 %all-reduce = (f32[16]{0:T(128)S(1)}, f32[16]{0:T(128)S(1)}) all-reduce(f32[16]{0:T(128)S(1)} %get-tuple-element.6, f32[16]{0:T(128)S(1)} %get-tuple-element.5), channel_id=1, replica_groups=mesh['gx'=4,'yz'=8] {'gx'}, use_global_device_ids=true, to_apply=%region_3.0 | all-reduce | flops 32 | bytes 256 | tf_op jit(solution)/shard_map/psum | solution.py:60
  16.6 1.0 fusion.20
  17.6 32.0 %all_gather.9 = bf16[128,2304]{1,0:T(8,128)(2,1)S(1)} all-gather(bf16[16,2304]{1,0:T(8,128)(2,1)S(1)} %fusion.20), channel_id=1, replica_groups=mesh['gx'=4,'yz'=8] {'yz'}, dimensions={0}, use_global_device_ids=true | all-gather | bytes 663552 | tf_op jit(solution)/shard_map/all_gather | solution.py:70
  49.6 0.0 copy-done
  49.6 0.9 fusion.29
  50.5 0.0 reduce-scatter.8.cloned.1.call-update
  50.5 0.0 reduce-scatter.6.cloned.1.call-start
  50.6 5.0 %fusion.28 = f32[128,1536]{1,0:T(8,128)} fusion(bf16[128,2304]{1,0:T(8,128)(2,1)S(1)} %all_gather.9, bf16[2304,1536]{1,0:T(8,128)(2,1)} %param.12), kind=kOutput, calls=%fused_computation.38 | convolution fusion | flops 905969664 | bytes 8454144 | tf_op jit(solution)/shard_map/dot_general | solution.py:71
  55.6 0.0 reduce-scatter.6.cloned.1.call-update
  55.6 0.0 reduce-scatter.12.cloned.1.call-start
  55.6 11.4 %fusion.31 = f32[128,4608]{1,0:T(8,128)} fusion(bf16[128,2304]{1,0:T(8,128)(2,1)S(1)} %all_gather.9, bf16[2304,4608]{1,0:T(8,128)(2,1)} %param.16), kind=kOutput, calls=%fused_computation.41 | convolution fusion | flops 2717908992 | bytes 24182784 | tf_op jit(solution)/shard_map/dot_general | solution.py:89
  67.1 0.0 reduce-scatter.12.cloned.1.call-update
  67.1 0.0 reduce-scatter.10.cloned.1.call-start
  67.2 11.4 %fusion.30 = f32[128,4608]{1,0:T(8,128)} fusion(bf16[128,2304]{1,0:T(8,128)(2,1)S(1)} %all_gather.9, bf16[2304,4608]{1,0:T(8,128)(2,1)} %param.15), kind=kOutput, calls=%fused_computation.40 | convolution fusion | flops 2717908992 | bytes 24182784 | tf_op jit(solution)/shard_map/dot_general | solution.py:88
  78.5 0.0 copy-start.2
  78.5 0.0 reduce-scatter.10.cloned.1.call-update
  78.6 0.0 reduce-scatter.8.cloned.1.call-done
  78.6 0.7 convert_element_type.40
  79.3 0.7 reshape.47
  80.0 5.4 %all-to-all-start.1 = ((bf16[8,2,128]{2,1,0:T(2,128)(2,1)}), bf16[8,2,128]{2,1,0:T(2,128)(2,1)S(1)}, u32[]{:S(2)}, u32[]{:S(2)}) async-start(bf16[8,2,128]{2,1,0:T(2,128)(2,1)} %reshape.47), calls=%async_computation.3 | async-start | bytes 8192 | tf_op jit(solution)/shard_map/all_to_all | solution.py:81
  85.4 0.0 copy-done.2
  85.4 0.1 iota_compare_fusion
  85.4 6.3 %all-to-all-done.1 = bf16[8,2,128]{2,1,0:T(2,128)(2,1)S(1)} async-done(((bf16[8,2,128]{2,1,0:T(2,128)(2,1)}), bf16[8,2,128]{2,1,0:T(2,128)(2,1)S(1)}, u32[]{:S(2)}, u32[]{:S(2)}) %all-to-all-start.1) | async-done | bytes 4128 | tf_op jit(solution)/shard_map/all_to_all | solution.py:81
  91.8 0.1 reshape.48
  91.8 0.1 all_to_all.46
  91.9 4.2 %reduce-scatter.6.cloned.1.call-done = f32[32,1536]{1,0:T(8,128)} async-done(((f32[128,1536]{1,0:T(8,128)}), f32[32,1536]{1,0:T(8,128)}) %reduce-scatter.6.cloned.1.call-update) | async-done | bytes 196624 | tf_op jit(solution)/shard_map/reduce_scatter | solution.py:74
  96.1 0.9 convert_element_type.39
  97.1 0.7 all_to_all.40
  97.7 5.5 %all-to-all-start = ((bf16[8,4,1536]{2,1,0:T(4,128)(2,1)}), bf16[8,4,1536]{2,1,0:T(4,128)(2,1)S(1)}, u32[]{:S(2)}, u32[]{:S(2)}) async-start(bf16[8,4,1536]{2,1,0:T(4,128)(2,1)} %all_to_all.40), calls=%async_computation.1 | async-start | bytes 196608 | tf_op jit(solution)/shard_map/all_to_all | solution.py:78
  103.2 0.0 all-gather.2.cloned.1.call-start
  103.3 7.1 %all-to-all-done = bf16[8,4,1536]{2,1,0:T(4,128)(2,1)S(1)} async-done(((bf16[8,4,1536]{2,1,0:T(4,128)(2,1)}), bf16[8,4,1536]{2,1,0:T(4,128)(2,1)S(1)}, u32[]{:S(2)}, u32[]{:S(2)}) %all-to-all-start) | async-done | bytes 98336 | tf_op jit(solution)/shard_map/all_to_all | solution.py:78
  110.4 0.1 reshape.44
  110.5 0.1 fusion.22
  110.6 21.2 %reduce-scatter.12.cloned.1.call-done = f32[32,4608]{1,0:T(8,128)} async-done(((f32[128,4608]{1,0:T(8,128)}), f32[32,4608]{1,0:T(8,128)}) %reduce-scatter.12.cloned.1.call-update) | async-done | bytes 589840 | tf_op jit(solution)/shard_map/reduce_scatter | solution.py:92
  131.8 35.7 %reduce-scatter.10.cloned.1.call-done = f32[32,4608]{1,0:T(8,128)} async-done(((f32[128,4608]{1,0:T(8,128)}), f32[32,4608]{1,0:T(8,128)}) %reduce-scatter.10.cloned.1.call-update) | async-done | bytes 589840 | tf_op jit(solution)/shard_map/reduce_scatter | solution.py:91
  167.5 2.1 multiply_convert_fusion
  169.6 0.0 all-gather.2.cloned.1.call-update
  169.6 0.0 reduce-scatter.14.cloned.1.call-start
  169.7 3.0 %select_reduce_fusion = (f32[4,48]{1,0:T(4,128)S(1)}, f32[4,48,1536]{2,1,0:T(8,128)S(1)}) fusion(f32[4,48]{1,0:T(4,128)S(1)} %broadcast_multiply_fusion, pred[4,1536]{1,0:T(4,128)(4,1)S(1)} %iota_compare_fusion, bf16[4,48,256]{2,1,0:T(8,128)(2,1)S(1)} %reshape.44, bf16[4,1536,512]{2,1,0:T(8,128)(2,1)} %param.18), kind=kOutput, calls=%fused_computation.8 | convolution fusion | flops 151879488 | bytes 4431360 | tf_op jit(solution)/shard_map/tgb,twb->tgw/dot_general | solution.py:22
  172.7 0.4 fusion.13
  173.1 2.6 fusion.10
  175.8 0.1 all_to_all.47
  175.9 0.1 copy.17
  175.9 12.4 %all_to_all.54 = bf16[4,8,1536]{2,0,1:T(4,128)(2,1)S(1)} all-to-all(bf16[4,8,1536]{2,0,1:T(4,128)(2,1)S(1)} %copy.17), channel_id=1, replica_groups=mesh['gx'=4,'yz'=8] {'yz'}, dimensions={1} | all-to-all | bytes 196608 | tf_op jit(solution)/shard_map/all_to_all | solution.py:86
  188.4 6.3 %all_gather.10 = bf16[128,1536]{1,0:T(8,128)(2,1)S(1)} all-gather(bf16[32,1536]{1,0:T(8,128)(2,1)S(1)} %all_to_all.50), channel_id=1, replica_groups=mesh['gx'=4,'yz'=8] {'gx'}, dimensions={0}, use_global_device_ids=true | all-gather | bytes 491520 | tf_op jit(solution)/shard_map/all_gather | solution.py:87
  194.7 0.0 all-gather.2.cloned.1.call-done
  194.7 9.1 %fusion.32 = f32[128,2304]{1,0:T(8,128)S(1)} fusion(bf16[128,4608]{1,0:T(8,128)(2,1)} %all-gather.2.cloned.1.call-done, bf16[4608,2304]{1,0:T(8,128)(2,1)} %param.17), kind=kOutput, calls=%fused_computation.42 | convolution fusion | flops 2717908992 | bytes 23592960 | tf_op jit(solution)/shard_map/dot_general | solution.py:98
  203.8 0.0 copy-start.1
  203.8 5.2 %convolution_add_fusion = f32[128,2304]{1,0:T(8,128)} fusion(f32[128,2304]{1,0:T(8,128)S(1)} %fusion.32, bf16[128,1536]{1,0:T(8,128)(2,1)S(1)} %all_gather.10, bf16[1536,2304]{1,0:T(8,128)(2,1)} %param.14), kind=kOutput, calls=%fused_computation | convolution fusion | flops 906264576 | bytes 9830400 | tf_op jit(solution)/shard_map/dot_general | solution.py:96
  209.0 0.0 reduce-scatter.14.cloned.1.call-update
  209.0 61.2 %reduce-scatter.14.cloned.1.call-done = f32[16,2304]{1,0:T(8,128)} async-done(((f32[128,2304]{1,0:T(8,128)}), f32[16,2304]{1,0:T(8,128)}) %reduce-scatter.14.cloned.1.call-update) | async-done | bytes 147472 | tf_op jit(solution)/shard_map/reduce_scatter | solution.py:97
  270.2 1.6 convert_element_type.47
  271.7 0.0 copy-done.1
  (8 shorter events, 0.1 us)
Async XLA Ops:
  6.5 43.0 %copy-start = (bf16[2304,64]{0,1:T(8,128)(2,1)S(1)}, bf16[2304,64]{0,1:T(8,128)(2,1)}, u32[]{:S(2)}) copy-start(bf16[2304,64]{0,1:T(8,128)(2,1)} %param.13) | copy-start | bytes 884740
  6.5 72.0 %reduce-scatter.8.cloned.1.call-start = ((), (), s32[]{:S(2)}) async-start(), calls=%async_computation.9 | async-start | bytes 81920 | tf_op jit(solution)/shard_map/reduce_scatter | solution.py:75
  50.5 45.6 %reduce-scatter.6.cloned.1.call-start = ((), (), s32[]{:S(2)}) async-start(), calls=%async_computation.8 | async-start | bytes 983040 | tf_op jit(solution)/shard_map/reduce_scatter | solution.py:74
  55.6 76.2 %reduce-scatter.12.cloned.1.call-start = ((), (), s32[]{:S(2)}) async-start(), calls=%async_computation.11 | async-start | bytes 2949120 | tf_op jit(solution)/shard_map/reduce_scatter | solution.py:92
  67.1 100.4 %reduce-scatter.10.cloned.1.call-start = ((), (), s32[]{:S(2)}) async-start(), calls=%async_computation.10 | async-start | bytes 2949120 | tf_op jit(solution)/shard_map/reduce_scatter | solution.py:91
  78.5 6.8 %copy-start.2 = (s32[4]{0:T(128)S(1)}, s32[4]{0:T(128)}, u32[]{:S(2)}) copy-start(s32[4]{0:T(128)} %param.19) | copy-start | bytes 52
  80.0 11.8 %all-to-all-start.1 = ((bf16[8,2,128]{2,1,0:T(2,128)(2,1)}), bf16[8,2,128]{2,1,0:T(2,128)(2,1)S(1)}, u32[]{:S(2)}, u32[]{:S(2)}) async-start(bf16[8,2,128]{2,1,0:T(2,128)(2,1)} %reshape.47), calls=%async_computation.3 | async-start | bytes 8192 | tf_op jit(solution)/shard_map/all_to_all | solution.py:81
  97.7 12.6 %all-to-all-start = ((bf16[8,4,1536]{2,1,0:T(4,128)(2,1)}), bf16[8,4,1536]{2,1,0:T(4,128)(2,1)S(1)}, u32[]{:S(2)}, u32[]{:S(2)}) async-start(bf16[8,4,1536]{2,1,0:T(4,128)(2,1)} %all_to_all.40), calls=%async_computation.1 | async-start | bytes 196608 | tf_op jit(solution)/shard_map/all_to_all | solution.py:78
  103.2 91.5 %all-gather.2.cloned.1.call-start = ((), (), s32[]{:S(2)}) async-start(), calls=%async_computation.12 | async-start | bytes 1474560 | tf_op jit(solution)/shard_map/all_gather | solution.py:95
  169.6 100.5 %reduce-scatter.14.cloned.1.call-start = ((), (), s32[]{:S(2)}) async-start(), calls=%async_computation.13 | async-start | bytes 1327104 | tf_op jit(solution)/shard_map/reduce_scatter | solution.py:97
  203.8 67.9 %copy-start.1 = (bf16[2304,64]{0,1:T(8,128)(2,1)S(1)}, bf16[2304,64]{0,1:T(8,128)(2,1)}, u32[]{:S(2)}) copy-start(bf16[2304,64]{0,1:T(8,128)(2,1)} %param.13) | copy-start | bytes 884740
Sparse Core Ops, SparseCore 0:
  50.6 19.4 reduce-scatter.7
  72.8 23.2 reduce-scatter.5
  98.7 33.1 reduce-scatter.11
  134.4 33.0 reduce-scatter.9
  169.8 17.4 all-gather.1
  209.1 61.0 reduce-scatter.13
where the time goes:
time: 279 us
  waiting for transfers between devices  136 us (49%)
  blocking collectives  59.1 us (21%)
  matrix products  48.8 us (17%)
  between operations  13.6 us (5%)
  starting transfers between devices  11.1 us (4%)
  other arithmetic  8.58 us (3%)
    reduce_scatter x1, waiting for transfers between devices, body(): lax.psum_scatter(first + jnp.dot(hidden, down_weight, preferred_element_t...  61.2 us
    reduce_scatter x1, waiting for transfers between devices, body(): lax.psum_scatter(gate_part, 'gx', scatter_dimension=0, tiled=True)  35.7 us
    all_gather x1, blocking collectives, body(): gathered = lax.all_gather(normed, 'yz', axis=0, tiled=True)  32 us
    reduce_scatter x1, waiting for transfers between devices, body(): lax.psum_scatter(up_part, 'gx', scatter_dimension=0, tiled=True)  21.2 us
    all_to_all x1, blocking collectives, body(): lax.all_to_all(attended, 'yz', split_axis=1, concat_axis=0, tiled=True)  12.4 us
    dot_general x1, matrix products, body(): up_part = jnp.dot(gathered, up_weight, preferred_element_type=jnp.float32)  11.4 us
    dot_general x1, matrix products, body(): jnp.dot(gathered, gate_weight, preferred_element_type=jnp.float32)  11.4 us
    dot_general x1, matrix products, body(): jnp.dot(hidden, down_weight, preferred_element_type=jnp.float32)  9.09 us
  transfers between devices with their start and end apart: 8, of which 6 were waited for; matrix products, arithmetic and copies ran while one was open for 13% of the time, Pallas kernels for 0%

commit v1 on v0

v1 whole, which is shorter than its diff:
```python
import functools
import math

import jax
import jax.numpy as jnp
from jax import lax
from jax.experimental import pallas as pl
from jax.experimental.pallas import tpu as pltpu
from jax.sharding import PartitionSpec as P

D = 9216
BF = jnp.bfloat16
F32 = jnp.float32
MESH = pl.DeviceIdType.MESH


def greet(peers):
    barrier = pltpu.get_barrier_semaphore()
    for peer in peers:
        pl.semaphore_signal(barrier, inc=1, device_id=peer, device_id_type=MESH)
    pl.semaphore_wait(barrier, len(peers))


def remote(src, dst, send, recv, peer):
    return pltpu.make_async_remote_copy(
        src_ref=src, dst_ref=dst, send_sem=send, recv_sem=recv,
        device_id=peer, device_id_type=MESH,
    )


class Pairs:
    def __init__(self, axis, n):
        self.axis, self.n, self.half = axis, n, n // 2
        self.me = lax.axis_index(axis)
        self.place = lax.rem(self.me, 2)
        self.row = lax.div(self.me, 2)
        self.partner = {axis: self.me + 1 - 2 * self.place}

    def ahead(self, j):
        return lax.rem(self.row + 1 + j, self.half)

    def behind(self, j):
        return lax.rem(self.row + 2 * self.half - 1 - j, self.half)

    def peer(self, j):
        return {self.axis: 2 * self.ahead(j) + self.place}

    def all(self):
        return [self.partner] + [self.peer(j) for j in range(self.half - 1)]


def gather_start(t, src, out, sa, ra, sb, rb):
    copies = []
    for j in range(t.half - 1):
        c = remote(src, out.at[t.me], sa.at[j], ra.at[j], t.peer(j))
        c.start()
        copies.append(c)
    c = remote(src, out.at[t.me], sb.at[0], rb.at[0], t.partner)
    c.start()
    return copies, [c]


def gather_finish(t, out, sa, ra, sb, rb, started):
    first, second = started
    for j in range(t.half - 1):
        got = 2 * t.behind(j) + t.place
        remote(out.at[got], out.at[got], sa.at[j], ra.at[j], t.peer(j)).wait_recv()
        c = remote(out.at[got], out.at[got], sb.at[1 + j], rb.at[1 + j], t.partner)
        c.start()
        second.append(c)
    for c in first:
        c.wait_send()
    for c in second:
        c.wait()


def norm_kernel(ngx, nyz, x_ref, gain_ref, out_ref, stat, got, ss, sr, sa, ra, sb, rb):
    gx = lax.axis_index("gx")
    t = Pairs("yz", nyz)
    others = [{"gx": lax.rem(gx + 1 + j, ngx)} for j in range(ngx - 1)]
    rows = x_ref.shape[0]
    x = x_ref[...].astype(F32)
    stat[0] = jnp.broadcast_to(jnp.sum(x, axis=1, keepdims=True), (rows, 128))
    stat[1] = jnp.broadcast_to(jnp.sum(x * x, axis=1, keepdims=True), (rows, 128))
    greet(others + t.all())
    copies = []
    for j in range(ngx - 1):
        c = remote(stat, got.at[j], ss.at[j], sr.at[j], others[j])
        c.start()
        copies.append(c)
    for c in copies:
        c.wait()
    total = stat[0]
    squares = stat[1]
    for j in range(ngx - 1):
        total = total + got[j, 0]
        squares = squares + got[j, 1]
    mean = total[:, :1] / D
    var = squares[:, :1] / D - mean * mean
    normed = (x - mean) * lax.rsqrt(var + 1e-05) * gain_ref[...].astype(F32)
    out_ref[t.me] = normed.astype(BF)
    started = gather_start(t, out_ref.at[t.me], out_ref, sa, ra, sb, rb)
    gather_finish(t, out_ref, sa, ra, sb, rb, started)


DMA = pltpu.SemaphoreType.DMA
VM = pl.BlockSpec(memory_space=pltpu.VMEM)


def params(cid):
    return pltpu.CompilerParams(
        collective_id=cid, has_side_effects=True, vmem_limit_bytes=48 * 1024 * 1024
    )


def norm_gather(x, gain, ngx, nyz):
    rows, cols = x.shape
    h = nyz // 2
    out = pl.pallas_call(
        functools.partial(norm_kernel, ngx, nyz),
        out_shape=jax.ShapeDtypeStruct((nyz, rows, cols), BF),
        in_specs=[VM, VM],
        out_specs=VM,
        scratch_shapes=[
            pltpu.VMEM((2, rows, 128), F32),
            pltpu.VMEM((ngx - 1, 2, rows, 128), F32),
            DMA((ngx - 1,)), DMA((ngx - 1,)),
            DMA((max(h - 1, 1),)), DMA((max(h - 1, 1),)), DMA((h,)), DMA((h,)),
        ],
        compiler_params=params(0),
        name="norm_gather",
    )(x, gain.reshape(1, cols))
    return out.reshape(nyz * rows, cols)


def reduce_start(t, x_ref, recv1, s1, r1):
    copies = []
    for j in range(t.half):
        k = t.ahead(j)
        c = remote(x_ref.at[2 * k + 1 - t.place], recv1.at[j], s1.at[j], r1.at[j], t.partner)
        c.start()
        copies.append(c)
    return copies


def reduce_rest(t, x_ref, recv1, stage, recv2, s2, r2, first):
    second = []
    for j in range(t.half - 1):
        k = t.ahead(j)
        first[j].wait_recv()
        stage[j] = (x_ref[2 * k + t.place].astype(F32) + recv1[j].astype(F32)).astype(BF)
        c = remote(stage.at[j], recv2.at[j], s2.at[j], r2.at[j], t.peer(j))
        c.start()
        second.append(c)
    first[t.half - 1].wait_recv()
    total = x_ref[t.me].astype(F32) + recv1[t.half - 1].astype(F32)
    for j in range(t.half - 1):
        second[j].wait_recv()
        total = total + recv2[j].astype(F32)
    for c in first + second:
        c.wait_send()
    return total


def reduce_kernel(axis, n, x_ref, out_ref, recv1, stage, recv2, s1, r1, s2, r2):
    t = Pairs(axis, n)
    greet(t.all())
    first = reduce_start(t, x_ref, recv1, s1, r1)
    out_ref[...] = reduce_rest(t, x_ref, recv1, stage, recv2, s2, r2, first).astype(out_ref.dtype)


def reduce_scratch(n, r, c):
    h = n // 2
    g = max(h - 1, 1)
    return [
        pltpu.VMEM((h, r, c), BF), pltpu.VMEM((g, r, c), BF), pltpu.VMEM((g, r, c), BF),
        DMA((h,)), DMA((h,)), DMA((g,)), DMA((g,)),
    ]


def reduce_scatter(x, axis, n, cid, dtype):
    rows, cols = x.shape
    r = rows // n
    return pl.pallas_call(
        functools.partial(reduce_kernel, axis, n),
        out_shape=jax.ShapeDtypeStruct((r, cols), dtype),
        in_specs=[VM],
        out_specs=VM,
        scratch_shapes=reduce_scratch(n, r, cols),
        compiler_params=params(cid),
        name="reduce_" + axis + str(cid),
    )(x.reshape(n, r, cols))


def gated_kernel(n, x_ref, out_ref, recv1, stage, recv2, s1, r1, s2, r2, sa, ra, sb, rb):
    t = Pairs("gx", n)
    greet(t.all())
    first = reduce_start(t, x_ref, recv1, s1, r1)
    both = reduce_rest(t, x_ref, recv1, stage, recv2, s2, r2, first)
    w = both.shape[1] // 2
    out_ref[t.me] = (jax.nn.silu(both[:, :w]) * both[:, w:]).astype(BF)
    started = gather_start(t, out_ref.at[t.me], out_ref, sa, ra, sb, rb)
    gather_finish(t, out_ref, sa, ra, sb, rb, started)


def gated(x, n, cid):
    rows, cols = x.shape
    r, h = rows // n, n // 2
    g = max(h - 1, 1)
    out = pl.pallas_call(
        functools.partial(gated_kernel, n),
        out_shape=jax.ShapeDtypeStruct((n, r, cols // 2), BF),
        in_specs=[VM],
        out_specs=VM,
        scratch_shapes=reduce_scratch(n, r, cols) + [DMA((g,)), DMA((g,)), DMA((h,)), DMA((h,))],
        compiler_params=params(cid),
        name="gated",
    )(x.reshape(n, r, cols))
    return out.reshape(rows, cols // 2)


def swap_kernel(axis, n, x_ref, out_ref, ss, rs):
    me = lax.axis_index(axis)
    peers = [{axis: lax.rem(me + 1 + j, n)} for j in range(n - 1)]
    greet(peers)
    copies = []
    for j in range(n - 1):
        c = remote(x_ref.at[lax.rem(me + 1 + j, n)], out_ref.at[me], ss.at[j], rs.at[j], peers[j])
        c.start()
        copies.append(c)
    out_ref[me] = x_ref[me]
    for c in copies:
        c.wait()


def swap(x, axis, n, cid):
    return pl.pallas_call(
        functools.partial(swap_kernel, axis, n),
        out_shape=jax.ShapeDtypeStruct(x.shape, x.dtype),
        in_specs=[VM],
        out_specs=VM,
        scratch_shapes=[DMA((n - 1,)), DMA((n - 1,))],
        compiler_params=params(cid),
        name="swap_" + str(cid),
    )(x)


def gather_kernel(axis, n, x_ref, out_ref, sa, ra, sb, rb):
    t = Pairs(axis, n)
    greet(t.all())
    started = gather_start(t, x_ref, out_ref, sa, ra, sb, rb)
    out_ref[t.me] = x_ref[...]
    gather_finish(t, out_ref, sa, ra, sb, rb, started)


def gather(x, axis, n, cid):
    h = n // 2
    g = max(h - 1, 1)
    return pl.pallas_call(
        functools.partial(gather_kernel, axis, n),
        out_shape=jax.ShapeDtypeStruct((n,) + x.shape, x.dtype),
        in_specs=[VM],
        out_specs=VM,
        scratch_shapes=[DMA((g,)), DMA((g,)), DMA((h,)), DMA((h,))],
        compiler_params=params(cid),
        name="gather_" + str(cid),
    )(x)


def attend_local(query, new_kv, cache, lengths):
    seqs = query.shape[0]
    head_dim = cache.shape[2] // 2
    heads = query.shape[1] // head_dim
    query_vectors = query.reshape(seqs, heads, head_dim)
    key_rows = cache[:, :, :head_dim]
    value_rows = cache[:, :, head_dim:]
    new_key = new_kv[:, :head_dim]
    new_value = new_kv[:, head_dim:]
    score_scale = 1.0 / math.sqrt(head_dim)
    attention_logits = (
        jnp.einsum("tgb,twb->tgw", query_vectors, key_rows, preferred_element_type=jnp.float32)
        * score_scale
    )
    own = (
        jnp.einsum("shd,sd->sh", query_vectors, new_key, preferred_element_type=jnp.float32)
        * score_scale
    )
    positions = lax.broadcasted_iota(jnp.int32, (1, 1, cache.shape[1]), 2)
    valid = positions < lengths[:, None, None]
    top = jnp.maximum(jnp.max(jnp.where(valid, attention_logits, own[:, :, None]), axis=2), own)
    weights = jnp.where(valid, jnp.exp(attention_logits - top[:, :, None]), jnp.float32(0.0))
    own_weight = jnp.exp(own - top)
    denom = jnp.sum(weights, axis=2) + own_weight
    attention_probabilities = (weights / denom[:, :, None]).astype(jnp.bfloat16)
    own_prob = (own_weight / denom).astype(jnp.bfloat16)
    value_mixture = jnp.einsum(
        "aqc,acn->aqn", attention_probabilities, value_rows, preferred_element_type=jnp.float32
    )
    value_mixture = (
        value_mixture
        + own_prob.astype(jnp.float32)[:, :, None] * new_value.astype(jnp.float32)[:, None, :]
    )
    return value_mixture.astype(jnp.bfloat16).reshape(seqs, heads * head_dim)


def body(ngx, nyz, stream, ln_gain, q_weight, kv_weight, out_weight, gate_weight, up_weight,
         down_weight, cache, lengths):
    normed = norm_gather(stream, ln_gain, ngx, nyz)
    batch = normed.shape[0]
    qc, kc = q_weight.shape[1], kv_weight.shape[1]
    pad = -(qc + kc) % 128
    seqs = batch // ngx // nyz

    q_part = jnp.dot(normed, q_weight, preferred_element_type=F32).astype(BF)
    kv_part = jnp.dot(normed, kv_weight, preferred_element_type=F32).astype(BF)
    qkv = jnp.concatenate([q_part, kv_part, jnp.zeros((batch, pad), BF)], axis=1)
    qkv_block = reduce_scatter(qkv, "gx", ngx, 1, BF)
    qkv_own = swap(qkv_block.reshape(nyz, seqs, qc + kc + pad), "yz", nyz, 2)
    qkv_own = jnp.swapaxes(qkv_own, 0, 1)
    query_own = qkv_own[:, :, :qc].reshape(seqs, nyz * qc)
    kv_own = qkv_own[:, :, qc:qc + kc].reshape(seqs, nyz * kc)
    attended = attend_local(query_own, kv_own, cache, lengths)
    blocks = jnp.swapaxes(attended.reshape(seqs, nyz, qc), 0, 1)
    head_block = swap(blocks, "yz", nyz, 3).reshape(nyz * seqs, qc)
    head_all = gather(head_block, "gx", ngx, 4).reshape(batch, qc)

    gate_part = jnp.dot(normed, gate_weight, preferred_element_type=F32).astype(BF)
    up_part = jnp.dot(normed, up_weight, preferred_element_type=F32).astype(BF)
    hidden = gated(jnp.concatenate([gate_part, up_part], axis=1), ngx, 5)
    part = jnp.dot(head_all, out_weight, preferred_element_type=F32) + jnp.dot(
        hidden, down_weight, preferred_element_type=F32
    )
    update = reduce_scatter(part.astype(BF), "yz", nyz, 6, F32)
    return update.astype(BF)


def solution(mesh):
    ngx, nyz = mesh.shape["gx"], mesh.shape["yz"]
    return jax.shard_map(
        functools.partial(body, ngx, nyz),
        mesh=mesh,
        in_specs=(
            P("yz", "gx"),
            P("gx"),
            P("gx", "yz"),
            P("gx", "yz"),
            P("yz", "gx"),
            P("gx", "yz"),
            P("gx", "yz"),
            P("yz", "gx"),
            P(("gx", "yz"), None, None),
            P(("gx", "yz")),
        ),
        out_specs=P("yz", "gx"),
        check_vma=False,
    )
```

time: 279 us -> 134 us (0.48)
  waiting for transfers between devices: 136 us -> 0 us
  Pallas kernels: 0 us -> 88.3 us
  blocking collectives: 59.1 us -> 0 us
  between operations: 13.6 us -> 0.26 us
  starting transfers between devices: 11.1 us -> 0 us
  matrix products: 48.8 us -> 40.3 us
  other arithmetic: 8.58 us -> 2.07 us
    reduce_scatter x5 -> x0, waiting for transfers between devices: 122 us -> none  [the longest x1 61.2 us: body(): lax.psum_scatter(first + jnp.dot(hidden, down_weight, preferred_element_t...]
    pallas_call x0 -> x7, Pallas kernels: none -> 88.3 us  [the longest x1 27.5 us: gated(): pl.pallas_call(functools.partial(gated_kernel, n), out_shape=jax.ShapeDty...]
    all_gather x2 -> x0, blocking collectives: 38.3 us -> none  [the longest x1 32 us: body(): gathered = lax.all_gather(normed, 'yz', axis=0, tiled=True)]
    all_to_all x2 -> x0, waiting for transfers between devices: 13.4 us -> none  [the longest x1 7.07 us: body(): lax.all_to_all(query_block.astype(jnp.bfloat16), 'yz', split_axis=0, conc...]
    all_to_all x1 -> x0, blocking collectives: 12.4 us -> none  [body(): lax.all_to_all(attended, 'yz', split_axis=1, concat_axis=0, tiled=True)]
    all_to_all x2 -> x0, starting transfers between devices: 10.9 us -> none  [the longest x1 5.52 us: body(): lax.all_to_all(query_block.astype(jnp.bfloat16), 'yz', split_axis=0, conc...]
    dot_general x6, matrix products: 43 us -> 34.5 us  [the longest x1 9.96 us: body(): up_part = jnp.dot(normed, up_weight, preferred_element_type=F32).astype(BF)]
    psum x1 -> x0, blocking collectives: 8.31 us -> none  [body(): lax.psum((jnp.sum(values_f, axis=1), jnp.sum(values_f * values_f, axis=1)...]
  transfers between devices with their start and end apart: 8 -> 0, of which waited for: 6 -> 0; matrix products, arithmetic and copies ran while one was open for 13% -> 0% of each run, Pallas kernels for 0% -> 0%
where the time goes in v1:
time: 134 us; the launch traced here: 133 us
  Pallas kernels  88.3 us (66%)
  matrix products  40.3 us (30%)
  local copies, waits for them, and re-layouts  2.32 us (2%)
  other arithmetic  2.07 us (2%)
    pallas_call x1, Pallas kernels, gated(): pl.pallas_call(functools.partial(gated_kernel, n), out_shape=jax.ShapeDty...  27.5 us
    pallas_call x1, Pallas kernels, norm_gather(): pl.pallas_call(functools.partial(norm_kernel, ngx, nyz), out_shape=jax.Sh...  20.5 us
    pallas_call x2, Pallas kernels, reduce_scatter(): pl.pallas_call(functools.partial(reduce_kernel, axis, n), out_shape=jax.S...  19.6 us
    pallas_call x2, Pallas kernels, swap(): pl.pallas_call(functools.partial(swap_kernel, axis, n), out_shape=jax.Sha...  14.8 us
    dot_general x1, matrix products, body(): up_part = jnp.dot(normed, up_weight, preferred_element_type=F32).astype(BF)  9.96 us
    dot_general x1, matrix products, body(): jnp.dot(normed, gate_weight, preferred_element_type=F32).astype(BF)  9.96 us
    dot_general x1, matrix products, body(): jnp.dot(hidden, down_weight, preferred_element_type=F32)  9.09 us
    pallas_call x1, Pallas kernels, gather(): pl.pallas_call(functools.partial(gather_kernel, axis, n), out_shape=jax.S...  5.94 us

profile of v1, /device:TPU:0, one launch (start us, length us, event | category | flops | bytes accessed | tf_op | source)
XLA Modules:
  0.0 133.2 jit_solution(12428607402376152736)
XLA Ops:
  0.0 0.0 copy-start
  0.0 0.8 iota_compare_fusion
  0.8 0.7 reshape.56.gain_ref
  1.5 0.0 copy-start.2
  1.5 0.9 copy-done.2
  2.4 20.5 %norm_gather.1 = bf16[8,16,2304]{2,1,0:T(8,128)(2,1)S(1)} custom-call(bf16[16,2304]{1,0:T(8,128)(2,1)S(1)} %copy-done.2, bf16[1,2304]{1,0:T(2,128)(2,1)S(1)} %reshape.56.gain_ref), custom_call_target="tpu_custom_call" | custom-call | tf_op jit(solution)/shard_map/norm_gather/pallas_call | solution.py:119
  22.8 0.0 copy-done
  22.8 0.3 convolution_convert_fusion.3
  23.2 0.1 copy.16
  23.3 4.1 %convolution_convert_fusion.2 = bf16[128,1536]{1,0:T(8,128)(2,1)S(1)} fusion(bf16[128,2304]{1,0:T(8,128)(2,1)S(1)} %bitcast.29, bf16[2304,1536]{1,0:T(8,128)(2,1)} %param.12), kind=kOutput, calls=%fused_computation.9 | convolution fusion | flops 906166272 | bytes 8060928 | tf_op jit(solution)/shard_map/dot_general | solution.py:314
  27.4 0.1 concatenate.6
  27.5 5.4 %reduce_gx1.1 = bf16[32,1664]{1,0:T(8,128)(2,1)S(1)} custom-call(bf16[4,32,1664]{2,1,0:T(8,128)(2,1)S(1)} %bitcast.36), custom_call_target="tpu_custom_call" | custom-call | tf_op jit(solution)/shard_map/reduce_gx1/pallas_call | solution.py:184
  33.0 7.6 %swap_2.1 = bf16[8,4,1664]{2,1,0:T(4,128)(2,1)S(1)} custom-call(bf16[8,4,1664]{2,1,0:T(4,128)(2,1)S(1)} %reshape.59.x_ref), custom_call_target="tpu_custom_call" | custom-call | tf_op jit(solution)/shard_map/swap_2/pallas_call | solution.py:237
  40.7 0.1 reshape_reshape.6
  40.8 0.1 reshape.60
  40.9 0.1 fusion.19
  41.0 3.0 %select_reduce_fusion = (f32[4,48]{1,0:T(4,128)S(1)}, f32[4,48,1536]{2,1,0:T(8,128)S(1)}) fusion(f32[4,48]{1,0:T(4,128)S(1)} %broadcast_multiply_fusion, pred[4,1536]{1,0:T(4,128)(4,1)S(1)} %iota_compare_fusion, bf16[4,48,256]{2,1,0:T(8,128)(2,1)S(1)} %reshape_reshape.6, bf16[4,1536,512]{2,1,0:T(8,128)(2,1)} %param.18), kind=kOutput, calls=%fused_computation.13 | convolution fusion | flops 151879488 | bytes 4431360 | tf_op jit(solution)/shard_map/tgb,twb->tgw/dot_general | solution.py:281
  44.1 0.4 fusion.14
  44.5 2.6 %fusion.11 = bf16[4,48,256]{2,1,0:T(8,128)(2,1)S(1)} fusion(bf16[4,1536,512]{2,1,0:T(8,128)(2,1)} %param.18, f32[4,48,1536]{2,1,0:T(8,128)S(1)} %get-tuple-element.10, f32[4,48]{1,0:T(4,128)S(1)} %get-tuple-element.6, f32[4,48]{1,0:T(4,128)S(1)} %fusion.24, pred[4,1536]{1,0:T(4,128)(4,1)S(1)} %iota_compare_fusion, f32[4,256]{1,0:T(4,128)S(1)} %get-tuple-element.7, ...), kind=kOutput, calls=%fused_computation.15 | convolution fusion | flops 152322048 | bytes 4436224 | tf_op jit(solution)/shard_map/aqc,acn->aqn/dot_general | solution.py:296
  47.1 0.1 reshape_reshape.7
  47.2 0.1 copy.25
  47.3 7.2 %swap_3.1 = bf16[8,4,1536]{2,1,0:T(4,128)(2,1)S(1)} custom-call(bf16[8,4,1536]{2,1,0:T(4,128)(2,1)S(1)} %bitcast.39), custom_call_target="tpu_custom_call" | custom-call | tf_op jit(solution)/shard_map/swap_3/pallas_call | solution.py:237
  54.5 5.9 %gather_4.1 = bf16[4,32,1536]{2,1,0:T(8,128)(2,1)S(1)} custom-call(bf16[32,1536]{1,0:T(8,128)(2,1)S(1)} %reshape.61.x_ref), custom_call_target="tpu_custom_call" | custom-call | tf_op jit(solution)/shard_map/gather_4/pallas_call | solution.py:259
  60.5 10.0 %convolution_convert_fusion = bf16[128,4608]{1,0:T(8,128)(2,1)S(1)} fusion(bf16[128,2304]{1,0:T(8,128)(2,1)S(1)} %bitcast.30, bf16[2304,4608]{1,0:T(8,128)(2,1)} %param.16), kind=kOutput, calls=%fused_computation | convolution fusion | flops 2718498816 | bytes 23003136 | tf_op jit(solution)/shard_map/dot_general | solution.py:328
  70.4 10.0 %convolution_convert_fusion.1 = bf16[128,4608]{1,0:T(8,128)(2,1)S(1)} fusion(bf16[128,2304]{1,0:T(8,128)(2,1)S(1)} %bitcast.31, bf16[2304,4608]{1,0:T(8,128)(2,1)} %param.15), kind=kOutput, calls=%fused_computation.1 | convolution fusion | flops 2718498816 | bytes 23003136 | tf_op jit(solution)/shard_map/dot_general | solution.py:327
  80.4 0.2 pad_maximum_fusion
  80.6 0.0 slice-start
  80.6 27.5 %gated.1 = bf16[4,32,4608]{2,1,0:T(8,128)(2,1)S(1)} custom-call(bf16[4,32,9216]{2,1,0:T(8,128)(2,1)S(1)} %bitcast.32), custom_call_target="tpu_custom_call" | custom-call | tf_op jit(solution)/shard_map/gated/pallas_call | solution.py:210
  108.2 0.0 slice-start.1
  108.2 9.1 %fusion.25 = f32[128,2304]{1,0:T(8,128)S(1)} fusion(bf16[128,4608]{1,0:T(8,128)(2,1)S(1)} %bitcast.33, bf16[4608,2304]{1,0:T(8,128)(2,1)} %param.17), kind=kOutput, calls=%fused_computation.35 | convolution fusion | flops 2717908992 | bytes 23592960 | tf_op jit(solution)/shard_map/dot_general | solution.py:330
  117.3 0.0 slice-done
  117.3 0.0 slice-done.1
  117.3 0.0 copy-start.1
  117.3 1.1 fusion
  118.4 14.1 %reduce_yz6.1 = f32[16,2304]{1,0:T(8,128)S(1)} custom-call(bf16[8,16,2304]{2,1,0:T(8,128)(2,1)S(1)} %bitcast.35), custom_call_target="tpu_custom_call" | custom-call | tf_op jit(solution)/shard_map/reduce_yz6/pallas_call | solution.py:184
  132.6 0.6 convert_element_type.43
  133.2 0.0 copy-done.1
  (12 shorter events, 0.2 us)
Async XLA Ops:
  0.0 22.8 %copy-start = (bf16[2304,64]{0,1:T(8,128)(2,1)S(1)}, bf16[2304,64]{0,1:T(8,128)(2,1)}, u32[]{:S(2)}) copy-start(bf16[2304,64]{0,1:T(8,128)(2,1)} %param.13) | copy-start | bytes 884740
  1.5 0.9 copy-start.2
  80.6 36.6 %slice-start = ((s8[7077888]{0:T(1024)(128)(4,1)}), s8[4194304]{0:T(1024)(128)(4,1)S(1)}, s32[]{:S(2)}) async-start(s8[7077888]{0:T(1024)(128)(4,1)} %bitcast.40), calls=%async_computation | async-start | bytes 8388608
  108.2 9.1 %slice-start.1 = ((s8[7077888]{0:T(1024)(128)(4,1)}), s8[2883584]{0:T(1024)(128)(4,1)S(1)}, s32[]{:S(2)}) async-start(s8[7077888]{0:T(1024)(128)(4,1)} %bitcast.40), calls=%async_computation.1 | async-start | bytes 5767168
  117.3 15.9 %copy-start.1 = (bf16[2304,64]{0,1:T(8,128)(2,1)S(1)}, bf16[2304,64]{0,1:T(8,128)(2,1)}, u32[]{:S(2)}) copy-start(bf16[2304,64]{0,1:T(8,128)(2,1)} %param.13) | copy-start | bytes 884740

commit v2 on v1

--- a/solution.py
+++ b/solution.py
@@ -143,128 +143,300 @@
     return copies
 
 
-def reduce_rest(t, x_ref, recv1, stage, recv2, s2, r2, first):
-    second = []
-    for j in range(t.half - 1):
-        k = t.ahead(j)
-        first[j].wait_recv()
-        stage[j] = (x_ref[2 * k + t.place].astype(F32) + recv1[j].astype(F32)).astype(BF)
-        c = remote(stage.at[j], recv2.at[j], s2.at[j], r2.at[j], t.peer(j))
+class Reduce:
+    def __init__(self, t, x, recv1, stage, recv2, s1, r1, s2, r2):
+        self.t, self.x, self.recv1, self.stage, self.recv2 = t, x, recv1, stage, recv2
+        self.s1, self.r1, self.s2, self.r2 = s1, r1, s2, r2
+
+    def start(self):
+        self.first = reduce_start(self.t, self.x, self.recv1, self.s1, self.r1)
+
+    def pass_on(self):
+        t = self.t
+        self.second = []
+        for j in range(t.half - 1):
+            k = t.ahead(j)
+            self.first[j].wait_recv()
+            self.stage[j] = (
+                self.x[2 * k + t.place].astype(F32) + self.recv1[j].astype(F32)
+            ).astype(BF)
+            c = remote(self.stage.at[j], self.recv2.at[j], self.s2.at[j], self.r2.at[j], t.peer(j))
+            c.start()
+            self.second.append(c)
+
+    def total(self):
+        t = self.t
+        self.first[t.half - 1].wait_recv()
+        total = self.x[t.me].astype(F32) + self.recv1[t.half - 1].astype(F32)
+        for j in range(t.half - 1):
+            self.second[j].wait_recv()
+            total = total + self.recv2[j].astype(F32)
+        return total
+
+    def end(self):
+        for c in self.first + self.second:
+            c.wait_send()
+
+
+class Gather:
+    def __init__(self, t, view, sa, ra, sb, rb):
+        self.t, self.view = t, view
+        self.sa, self.ra, self.sb, self.rb = sa, ra, sb, rb
+
+    def start(self):
+        t, own = self.t, self.view(self.t.me)
+        self.first = []
+        for j in range(t.half - 1):
+            c = remote(own, own, self.sa.at[j], self.ra.at[j], t.peer(j))
+            c.start()
+            self.first.append(c)
+        c = remote(own, own, self.sb.at[0], self.rb.at[0], t.partner)
         c.start()
-        second.append(c)
-    first[t.half - 1].wait_recv()
-    total = x_ref[t.me].astype(F32) + recv1[t.half - 1].astype(F32)
-    for j in range(t.half - 1):
-        second[j].wait_recv()
-        total = total + recv2[j].astype(F32)
-    for c in first + second:
-        c.wait_send()
-    return total
-
-
-def reduce_kernel(axis, n, x_ref, out_ref, recv1, stage, recv2, s1, r1, s2, r2):
-    t = Pairs(axis, n)
-    greet(t.all())
-    first = reduce_start(t, x_ref, recv1, s1, r1)
-    out_ref[...] = reduce_rest(t, x_ref, recv1, stage, recv2, s2, r2, first).astype(out_ref.dtype)
-
-
-def reduce_scratch(n, r, c):
-    h = n // 2
+        self.second = [c]
+
+    def pass_on(self):
+        t = self.t
+        for j in range(t.half - 1):
+            got = self.view(2 * t.behind(j) + t.place)
+            remote(got, got, self.sa.at[j], self.ra.at[j], t.peer(j)).wait_recv()
+            c = remote(got, got, self.sb.at[1 + j], self.rb.at[1 + j], t.partner)
+            c.start()
+            self.second.append(c)
+
+    def end(self):
+        for c in self.first:
+            c.wait_send()
+        for c in self.second:
+            c.wait()
+
+
+class Swap:
+    def __init__(self, axis, n, src, dst, ss, rs):
+        self.me = lax.axis_index(axis)
+        self.n, self.src, self.dst, self.ss, self.rs = n, src, dst, ss, rs
+        self.ids = [lax.rem(self.me + 1 + j, n) for j in range(n - 1)]
+        self.peers = [{axis: i} for i in self.ids]
+
+    def start(self):
+        self.copies = []
+        for j in range(self.n - 1):
+            c = remote(
+                self.src.at[self.ids[j]], self.dst.at[self.me], self.ss.at[j], self.rs.at[j],
+                self.peers[j],
+            )
+            c.start()
+            self.copies.append(c)
+        self.dst[self.me] = self.src[self.me]
+
+    def end(self):
+        for c in self.copies:
+            c.wait()
+
+
+def first_kernel(ngx, nyz, w, x_ref, kv_ref, qw, gw, uw, hid, own,
+                 wbuf, wsem, qx, q1, qs, q2, qsem1, qsem2, qsem3, qsem4, sw, ssem, rsem,
+                 px, p1, ps, p2, psem1, psem2, psem3, psem4, sa, ra, sb, rb):
+    t = Pairs("gx", ngx)
+    qc, ff = qw.shape[1], gw.shape[1]
+    nq, nc = qc // w, ff // w
+    r = hid.shape[1]
+    slots = wbuf.shape[0]
+    tiles = [(qw, i) for i in range(nq)]
+    for c in range(nc):
+        tiles += [(gw, c), (uw, c)]
+
+    def fetch(i):
+        ref, c = tiles[i]
+        return pltpu.make_async_copy(ref.at[:, pl.ds(c * w, w)], wbuf.at[i % slots], wsem.at[i % slots])
+
+    for i in range(min(slots, len(tiles))):
+        fetch(i).start()
+    swap = Swap("yz", nyz, sw, own, ssem, rsem)
+    greet(t.all() + swap.peers)
+
+    jobs = {}
+
+    def at(step, f):
+        jobs.setdefault(step, []).append(f)
+
+    qred = Reduce(t, qx, q1, qs, q2, qsem1, qsem2, qsem3, qsem4)
+    reds = [
+        Reduce(t, px.at[c], p1.at[c], ps.at[c], p2.at[c], psem1.at[c], psem2.at[c], psem3.at[c], psem4.at[c])
+        for c in range(nc)
+    ]
+    gats = [
+        Gather(t, lambda i, c=c: hid.at[i, :, pl.ds(c * w, w)], sa.at[c], ra.at[c], sb.at[c], rb.at[c])
+        for c in range(nc)
+    ]
+
+    def q_total():
+        total = qred.total()
+        seqs = sw.shape[1]
+        for i in range(nyz):
+            sw[i] = total[i * seqs:(i + 1) * seqs].astype(BF)
+        swap.start()
+
+    def h_total(c):
+        both = reds[c].total()
+        hid[t.me, :, c * w:(c + 1) * w] = (jax.nn.silu(both[:, :w]) * both[:, w:]).astype(BF)
+        gats[c].start()
+
+    at(nq - 1, qred.start)
+    at(nq, qred.pass_on)
+    at(nq + 2, q_total)
+    for c in range(nc):
+        s = nq + 2 * c + 1
+        at(s, reds[c].start)
+        at(s + 1, reds[c].pass_on)
+        at(s + 3, lambda c=c: h_total(c))
+        at(s + 5, gats[c].pass_on)
+
+    x = x_ref[...]
+    for i in range(max(jobs) + 1):
+        if i < len(tiles):
+            fetch(i).wait()
+            y = jnp.dot(x, wbuf[i % slots], preferred_element_type=F32).astype(BF).reshape(ngx, r, w)
+            if i < nq:
+                qx[:, :, i * w:(i + 1) * w] = y
+            else:
+                side = (i - nq) % 2
+                px[(i - nq) // 2, :, :, side * w:(side + 1) * w] = y
+            if i + slots < len(tiles):
+                fetch(i + slots).start()
+            if i == nq - 1:
+                qx[:, :, qc:] = kv_ref[...].reshape(ngx, r, kv_ref.shape[1])
+        for f in jobs.get(i, []):
+            f()
+    for c in range(nc):
+        reds[c].end()
+        gats[c].end()
+    qred.end()
+    swap.end()
+
+
+def first(x, kv, qw, gw, uw, ngx, nyz):
+    batch, depth = x.shape
+    qc, ff = qw.shape[1], gw.shape[1]
+    w = 768 if qc % 768 == 0 and ff % 768 == 0 else 384
+    nc = ff // w
+    r, h = batch // ngx, ngx // 2
     g = max(h - 1, 1)
-    return [
-        pltpu.VMEM((h, r, c), BF), pltpu.VMEM((g, r, c), BF), pltpu.VMEM((g, r, c), BF),
-        DMA((h,)), DMA((h,)), DMA((g,)), DMA((g,)),
+    seqs = r // nyz
+    width = qc + kv.shape[1]
+    slots = 4
+    ANY = pl.BlockSpec(memory_space=pl.ANY)
+    return pl.pallas_call(
+        functools.partial(first_kernel, ngx, nyz, w),
+        out_shape=[
+            jax.ShapeDtypeStruct((ngx, r, ff), BF),
+            jax.ShapeDtypeStruct((nyz, seqs, width), BF),
+        ],
+        in_specs=[VM, VM, ANY, ANY, ANY],
+        out_specs=[VM, VM],
+        scratch_shapes=[
+            pltpu.VMEM((slots, depth, w), BF), DMA((slots,)),
+            pltpu.VMEM((ngx, r, width), BF), pltpu.VMEM((h, r, width), BF),
+            pltpu.VMEM((g, r, width), BF), pltpu.VMEM((g, r, width), BF),
+            DMA((h,)), DMA((h,)), DMA((g,)), DMA((g,)),
+            pltpu.VMEM((nyz, seqs, width), BF), DMA((nyz - 1,)), DMA((nyz - 1,)),
+            pltpu.VMEM((nc, ngx, r, 2 * w), BF), pltpu.VMEM((nc, h, r, 2 * w), BF),
+            pltpu.VMEM((nc, g, r, 2 * w), BF), pltpu.VMEM((nc, g, r, 2 * w), BF),
+            DMA((nc, h)), DMA((nc, h)), DMA((nc, g)), DMA((nc, g)),
+            DMA((nc, g)), DMA((nc, g)), DMA((nc, h)), DMA((nc, h)),
+        ],
+        compiler_params=params(1),
+        name="project",
+    )(x, kv, qw, gw, uw)
+
+
+def second_kernel(ngx, nyz, wd, wo, hid_ref, att_ref, dw, ow, out_ref,
+                  dbuf, dsem, obuf, osem, acc, sw, ssem, rsem, heads, sa, ra, sb, rb,
+                  px, p1, ps, p2, psem1, psem2, psem3, psem4):
+    tx, ty = Pairs("gx", ngx), Pairs("yz", nyz)
+    cols = dw.shape[1]
+    nd, no = cols // wd, cols // wo
+    r, qc = heads.shape[1], heads.shape[2]
+    seqs = att_ref.shape[1]
+    slots = dbuf.shape[0]
+
+    def fetch(i):
+        return pltpu.make_async_copy(dw.at[:, pl.ds(i * wd, wd)], dbuf.at[i % slots], dsem.at[i % slots])
+
+    def fetch_out(i):
+        return pltpu.make_async_copy(ow.at[:, pl.ds(i * wo, wo)], obuf.at[i], osem.at[i])
+
+    for i in range(min(slots, nd)):
+        fetch(i).start()
+    swap = Swap("yz", nyz, att_ref, sw, ssem, rsem)
+    greet(tx.all() + swap.peers)
+    swap.start()
+    gat = Gather(tx, lambda i: heads.at[i], sa, ra, sb, rb)
+
+    def join():
+        swap.end()
+        heads[tx.me] = jnp.concatenate([sw[i].astype(F32) for i in range(nyz)], axis=0).astype(BF)
+        gat.start()
+
+    jobs = {2: join, 5: gat.pass_on}
+    hid = hid_ref[...]
+    for i in range(nd):
+        fetch(i).wait()
+        acc[:, i * wd:(i + 1) * wd] = jnp.dot(hid, dbuf[i % slots], preferred_element_type=F32)
+        if i + slots < nd:
+            fetch(i + slots).start()
+        elif i + slots - nd < no:
+            fetch_out(i + slots - nd).start()
+        if i in jobs:
+            jobs[i]()
+    gat.end()
+    att = heads[...].reshape(ngx * r, qc)
+    reds = [
+        Reduce(ty, px.at[c], p1.at[c], ps.at[c], p2.at[c], psem1.at[c], psem2.at[c], psem3.at[c], psem4.at[c])
+        for c in range(no)
     ]
-
-
-def reduce_scatter(x, axis, n, cid, dtype):
-    rows, cols = x.shape
-    r = rows // n
+    rows = out_ref.shape[0]
+    for c in range(no):
+        fetch_out(c).wait()
+        y = acc[:, c * wo:(c + 1) * wo] + jnp.dot(att, obuf[c], preferred_element_type=F32)
+        px[c] = y.astype(BF).reshape(nyz, rows, wo)
+        reds[c].start()
+        if c > 0:
+            reds[c - 1].pass_on()
+    reds[no - 1].pass_on()
+    for c in range(no):
+        out_ref[:, c * wo:(c + 1) * wo] = reds[c].total()
+    for c in range(no):
+        reds[c].end()
+
+
+def second(hid, att, dw, ow, ngx, nyz):
+    batch, ff = hid.shape
+    _, seqs, qc = att.shape
+    cols = dw.shape[1]
+    wd, wo = 256, 768
+    no = cols // wo
+    rx, r, hx, hy = batch // ngx, batch // nyz, ngx // 2, nyz // 2
+    gx, gy = max(hx - 1, 1), max(hy - 1, 1)
+    slots = 4
+    ANY = pl.BlockSpec(memory_space=pl.ANY)
     return pl.pallas_call(
-        functools.partial(reduce_kernel, axis, n),
-        out_shape=jax.ShapeDtypeStruct((r, cols), dtype),
-        in_specs=[VM],
+        functools.partial(second_kernel, ngx, nyz, wd, wo),
+        out_shape=jax.ShapeDtypeStruct((r, cols), F32),
+        in_specs=[VM, VM, ANY, ANY],
         out_specs=VM,
-        scratch_shapes=reduce_scratch(n, r, cols),
-        compiler_params=params(cid),
-        name="reduce_" + axis + str(cid),
-    )(x.reshape(n, r, cols))
-
-
-def gated_kernel(n, x_ref, out_ref, recv1, stage, recv2, s1, r1, s2, r2, sa, ra, sb, rb):
-    t = Pairs("gx", n)
-    greet(t.all())
-    first = reduce_start(t, x_ref, recv1, s1, r1)
-    both = reduce_rest(t, x_ref, recv1, stage, recv2, s2, r2, first)
-    w = both.shape[1] // 2
-    out_ref[t.me] = (jax.nn.silu(both[:, :w]) * both[:, w:]).astype(BF)
-    started = gather_start(t, out_ref.at[t.me], out_ref, sa, ra, sb, rb)
-    gather_finish(t, out_ref, sa, ra, sb, rb, started)
-
-
-def gated(x, n, cid):
-    rows, cols = x.shape
-    r, h = rows // n, n // 2
-    g = max(h - 1, 1)
-    out = pl.pallas_call(
-        functools.partial(gated_kernel, n),
-        out_shape=jax.ShapeDtypeStruct((n, r, cols // 2), BF),
-        in_specs=[VM],
-        out_specs=VM,
-        scratch_shapes=reduce_scratch(n, r, cols) + [DMA((g,)), DMA((g,)), DMA((h,)), DMA((h,))],
-        compiler_params=params(cid),
-        name="gated",
-    )(x.reshape(n, r, cols))
-    return out.reshape(rows, cols // 2)
-
-
-def swap_kernel(axis, n, x_ref, out_ref, ss, rs):
-    me = lax.axis_index(axis)
-    peers = [{axis: lax.rem(me + 1 + j, n)} for j in range(n - 1)]
-    greet(peers)
-    copies = []
-    for j in range(n - 1):
-        c = remote(x_ref.at[lax.rem(me + 1 + j, n)], out_ref.at[me], ss.at[j], rs.at[j], peers[j])
-        c.start()
-        copies.append(c)
-    out_ref[me] = x_ref[me]
-    for c in copies:
-        c.wait()
-
-
-def swap(x, axis, n, cid):
-    return pl.pallas_call(
-        functools.partial(swap_kernel, axis, n),
-        out_shape=jax.ShapeDtypeStruct(x.shape, x.dtype),
-        in_specs=[VM],
-        out_specs=VM,
-        scratch_shapes=[DMA((n - 1,)), DMA((n - 1,))],
-        compiler_params=params(cid),
-        name="swap_" + str(cid),
-    )(x)
-
-
-def gather_kernel(axis, n, x_ref, out_ref, sa, ra, sb, rb):
-    t = Pairs(axis, n)
-    greet(t.all())
-    started = gather_start(t, x_ref, out_ref, sa, ra, sb, rb)
-    out_ref[t.me] = x_ref[...]
-    gather_finish(t, out_ref, sa, ra, sb, rb, started)
-
-
-def gather(x, axis, n, cid):
-    h = n // 2
-    g = max(h - 1, 1)
-    return pl.pallas_call(
-        functools.partial(gather_kernel, axis, n),
-        out_shape=jax.ShapeDtypeStruct((n,) + x.shape, x.dtype),
-        in_specs=[VM],
-        out_specs=VM,
-        scratch_shapes=[DMA((g,)), DMA((g,)), DMA((h,)), DMA((h,))],
-        compiler_params=params(cid),
-        name="gather_" + str(cid),
-    )(x)
+        scratch_shapes=[
+            pltpu.VMEM((slots, ff, wd), BF), DMA((slots,)),
+            pltpu.VMEM((no, qc, wo), BF), DMA((no,)),
+            pltpu.VMEM((batch, cols), F32),
+            pltpu.VMEM((nyz, seqs, qc), BF), DMA((nyz - 1,)), DMA((nyz - 1,)),
+            pltpu.VMEM((ngx, rx, qc), BF), DMA((gx,)), DMA((gx,)), DMA((hx,)), DMA((hx,)),
+            pltpu.VMEM((no, nyz, r, wo), BF), pltpu.VMEM((no, hy, r, wo), BF),
+            pltpu.VMEM((no, gy, r, wo), BF), pltpu.VMEM((no, gy, r, wo), BF),
+            DMA((no, hy)), DMA((no, hy)), DMA((no, gy)), DMA((no, gy)),
+        ],
+        compiler_params=params(2),
+        name="combine",
+    )(hid, att, dw, ow)
 
 
 def attend_local(query, new_kv, cache, lengths):
@@ -311,26 +483,15 @@
     pad = -(qc + kc) % 128
     seqs = batch // ngx // nyz
 
-    q_part = jnp.dot(normed, q_weight, preferred_element_type=F32).astype(BF)
     kv_part = jnp.dot(normed, kv_weight, preferred_element_type=F32).astype(BF)
-    qkv = jnp.concatenate([q_part, kv_part, jnp.zeros((batch, pad), BF)], axis=1)
-    qkv_block = reduce_scatter(qkv, "gx", ngx, 1, BF)
-    qkv_own = swap(qkv_block.reshape(nyz, seqs, qc + kc + pad), "yz", nyz, 2)
+    kv_part = jnp.pad(kv_part, ((0, 0), (0, pad)))
+    hidden, qkv_own = first(normed, kv_part, q_weight, gate_weight, up_weight, ngx, nyz)
     qkv_own = jnp.swapaxes(qkv_own, 0, 1)
     query_own = qkv_own[:, :, :qc].reshape(seqs, nyz * qc)
     kv_own = qkv_own[:, :, qc:qc + kc].reshape(seqs, nyz * kc)
     attended = attend_local(query_own, kv_own, cache, lengths)
     blocks = jnp.swapaxes(attended.reshape(seqs, nyz, qc), 0, 1)
-    head_block = swap(blocks, "yz", nyz, 3).reshape(nyz * seqs, qc)
-    head_all = gather(head_block, "gx", ngx, 4).reshape(batch, qc)
-
-    gate_part = jnp.dot(normed, gate_weight, preferred_element_type=F32).astype(BF)
-    up_part = jnp.dot(normed, up_weight, preferred_element_type=F32).astype(BF)
-    hidden = gated(jnp.concatenate([gate_part, up_part], axis=1), ngx, 5)
-    part = jnp.dot(head_all, out_weight, preferred_element_type=F32) + jnp.dot(
-        hidden, down_weight, preferred_element_type=F32
-    )
-    update = reduce_scatter(part.astype(BF), "yz", nyz, 6, F32)
+    update = second(hidden.reshape(batch, -1), blocks, down_weight, out_weight, ngx, nyz)
     return update.astype(BF)
 
 

time: 134 us -> 98.6 us (0.74)
  matrix products: 40.3 us -> 6.05 us
    dot_general x5 -> x0, matrix products: 34.2 us -> none  [the longest x1 9.96 us: body(): up_part = jnp.dot(normed, up_weight, preferred_element_type=F32).astype(BF)]
    pallas_call x6 -> x2, Pallas kernels: 67.8 us -> 67.7 us  [the longest x1 43.3 us: first(): pl.pallas_call(functools.partial(first_kernel, ngx, nyz, w), out_shape=[j...]
where the time goes in v2:
time: 98.6 us; the launch traced here: 98.3 us
  Pallas kernels  88.1 us (89%)
  matrix products  6.05 us (6%)
  local copies, waits for them, and re-layouts  2.16 us (2%)
  other arithmetic  1.83 us (2%)
    pallas_call x1, Pallas kernels, first(): pl.pallas_call(functools.partial(first_kernel, ngx, nyz, w), out_shape=[j...  43.3 us
    pallas_call x1, Pallas kernels, second(): pl.pallas_call(functools.partial(second_kernel, ngx, nyz, wd, wo), out_sh...  24.4 us
    pallas_call x1, Pallas kernels, norm_gather(): pl.pallas_call(functools.partial(norm_kernel, ngx, nyz), out_shape=jax.Sh...  20.5 us
    dot_general x1, matrix products, attend_local(): jnp.einsum('tgb,twb->tgw', query_vectors, key_rows, preferred_element_typ...  3.03 us
    dot_general x1, matrix products, attend_local(): jnp.einsum('aqc,acn->aqn', attention_probabilities, value_rows, preferred...  2.6 us

profile of v2, /device:TPU:0, one launch (start us, length us, event | category | flops | bytes accessed | tf_op | source)
XLA Modules:
  0.0 98.3 jit_solution(2093306435214514258)
XLA Ops:
  0.0 0.0 copy-start
  0.0 0.8 iota_compare_fusion
  0.8 0.7 reshape.38.gain_ref
  1.5 0.0 copy-start.2
  1.5 0.9 copy-done.2
  2.4 20.5 %norm_gather.1 = bf16[8,16,2304]{2,1,0:T(8,128)(2,1)S(1)} custom-call(bf16[16,2304]{1,0:T(8,128)(2,1)S(1)} %copy-done.2, bf16[1,2304]{1,0:T(2,128)(2,1)S(1)} %reshape.38.gain_ref), custom_call_target="tpu_custom_call" | custom-call | tf_op jit(solution)/shard_map/norm_gather/pallas_call | solution.py:119
  22.8 0.0 copy-done
  22.8 0.3 convolution_convert_fusion
  23.1 0.1 copy.16
  23.3 43.3 %project.1 = (bf16[4,32,4608]{2,1,0:T(8,128)(2,1)S(1)}, bf16[8,4,1664]{2,1,0:T(4,128)(2,1)S(1)}) custom-call(bf16[128,2304]{1,0:T(8,128)(2,1)S(1)} %bitcast.15, bf16[128,128]{1,0:T(8,128)(2,1)S(1)} %pad.4.kv_ref, bf16[2304,1536]{1,0:T(8,128)(2,1)} %qw.1, bf16[2304,4608]{1,0:T(8,128)(2,1)} %gw.1, bf16[2304,4608]{1,0:T(8,128)(2,1)} %uw.1), custom_call_target="tpu_custom_call" | custom-call | tf_op jit(solution)/shard_map/project/pallas_call | solution.py:328
  66.7 0.1 reshape_reshape.6
  66.8 0.1 reshape.41
  66.9 0.1 fusion.18
  67.0 3.0 %select_reduce_fusion = (f32[4,48]{1,0:T(4,128)S(1)}, f32[4,48,1536]{2,1,0:T(8,128)S(1)}) fusion(f32[4,48]{1,0:T(4,128)S(1)} %broadcast_multiply_fusion, pred[4,1536]{1,0:T(4,128)(4,1)S(1)} %iota_compare_fusion, bf16[4,48,256]{2,1,0:T(8,128)(2,1)S(1)} %reshape_reshape.6, bf16[4,1536,512]{2,1,0:T(8,128)(2,1)} %param.18), kind=kOutput, calls=%fused_computation.7 | convolution fusion | flops 151879488 | bytes 4431360 | tf_op jit(solution)/shard_map/tgb,twb->tgw/dot_general | solution.py:453
  70.1 0.4 fusion.13
  70.5 2.6 %fusion.10 = bf16[4,48,256]{2,1,0:T(8,128)(2,1)S(1)} fusion(bf16[4,1536,512]{2,1,0:T(8,128)(2,1)} %param.18, f32[4,48,1536]{2,1,0:T(8,128)S(1)} %get-tuple-element.14, f32[4,48]{1,0:T(4,128)S(1)} %get-tuple-element.10, f32[4,48]{1,0:T(4,128)S(1)} %fusion.23, pred[4,1536]{1,0:T(4,128)(4,1)S(1)} %iota_compare_fusion, f32[4,256]{1,0:T(4,128)S(1)} %get-tuple-element.11, ...), kind=kOutput, calls=%fused_computation.9 | convolution fusion | flops 152322048 | bytes 4436224 | tf_op jit(solution)/shard_map/aqc,acn->aqn/dot_general | solution.py:468
  73.1 0.1 reshape_reshape.7
  73.2 0.1 copy.25
  73.2 0.0 copy-start.1
  73.2 24.4 %combine.1 = f32[16,2304]{1,0:T(8,128)S(1)} custom-call(bf16[128,4608]{1,0:T(8,128)(2,1)S(1)} %bitcast.16, bf16[8,4,1536]{2,1,0:T(4,128)(2,1)S(1)} %bitcast.17, bf16[4608,2304]{1,0:T(8,128)(2,1)} %dw.1, bf16[1536,2304]{1,0:T(8,128)(2,1)} %ow.1), custom_call_target="tpu_custom_call" | custom-call | tf_op jit(solution)/shard_map/combine/pallas_call | solution.py:422
  97.7 0.6 convert_element_type.29
  98.3 0.0 copy-done.1
  (9 shorter events, 0.1 us)
Async XLA Ops:
  0.0 22.8 %copy-start = (bf16[2304,64]{0,1:T(8,128)(2,1)S(1)}, bf16[2304,64]{0,1:T(8,128)(2,1)}, u32[]{:S(2)}) copy-start(bf16[2304,64]{0,1:T(8,128)(2,1)} %param.13) | copy-start | bytes 884740
  1.5 0.9 copy-start.2
  73.2 25.1 %copy-start.1 = (bf16[2304,64]{0,1:T(8,128)(2,1)S(1)}, bf16[2304,64]{0,1:T(8,128)(2,1)}, u32[]{:S(2)}) copy-start(bf16[2304,64]{0,1:T(8,128)(2,1)} %param.13) | copy-start | bytes 884740

commit v3 on v2

--- a/solution.py
+++ b/solution.py
@@ -74,17 +74,13 @@
         c.wait()
 
 
-def norm_kernel(ngx, nyz, x_ref, gain_ref, out_ref, stat, got, ss, sr, sa, ra, sb, rb):
-    gx = lax.axis_index("gx")
-    t = Pairs("yz", nyz)
-    others = [{"gx": lax.rem(gx + 1 + j, ngx)} for j in range(ngx - 1)]
+def normalize(t, others, x_ref, gain_ref, out_ref, stat, got, ss, sr, sa, ra, sb, rb):
     rows = x_ref.shape[0]
     x = x_ref[...].astype(F32)
     stat[0] = jnp.broadcast_to(jnp.sum(x, axis=1, keepdims=True), (rows, 128))
     stat[1] = jnp.broadcast_to(jnp.sum(x * x, axis=1, keepdims=True), (rows, 128))
-    greet(others + t.all())
     copies = []
-    for j in range(ngx - 1):
+    for j in range(len(others)):
         c = remote(stat, got.at[j], ss.at[j], sr.at[j], others[j])
         c.start()
         copies.append(c)
@@ -92,7 +88,7 @@
         c.wait()
     total = stat[0]
     squares = stat[1]
-    for j in range(ngx - 1):
+    for j in range(len(others)):
         total = total + got[j, 0]
         squares = squares + got[j, 1]
     mean = total[:, :1] / D
@@ -109,28 +105,8 @@
 
 def params(cid):
     return pltpu.CompilerParams(
-        collective_id=cid, has_side_effects=True, vmem_limit_bytes=48 * 1024 * 1024
-    )
-
-
-def norm_gather(x, gain, ngx, nyz):
-    rows, cols = x.shape
-    h = nyz // 2
-    out = pl.pallas_call(
-        functools.partial(norm_kernel, ngx, nyz),
-        out_shape=jax.ShapeDtypeStruct((nyz, rows, cols), BF),
-        in_specs=[VM, VM],
-        out_specs=VM,
-        scratch_shapes=[
-            pltpu.VMEM((2, rows, 128), F32),
-            pltpu.VMEM((ngx - 1, 2, rows, 128), F32),
-            DMA((ngx - 1,)), DMA((ngx - 1,)),
-            DMA((max(h - 1, 1),)), DMA((max(h - 1, 1),)), DMA((h,)), DMA((h,)),
-        ],
-        compiler_params=params(0),
-        name="norm_gather",
-    )(x, gain.reshape(1, cols))
-    return out.reshape(nyz * rows, cols)
+        collective_id=cid, has_side_effects=True, vmem_limit_bytes=52 * 1024 * 1024
+    )
 
 
 def reduce_start(t, x_ref, recv1, s1, r1):
@@ -233,7 +209,8 @@
             c.wait()
 
 
-def first_kernel(ngx, nyz, w, x_ref, kv_ref, qw, gw, uw, hid, own,
+def first_kernel(ngx, nyz, w, s_ref, gain_ref, kvw, qw, gw, uw, hid, own,
+                 xg, stat, got, nss, nsr, nsa, nra, nsb, nrb,
                  wbuf, wsem, qx, q1, qs, q2, qsem1, qsem2, qsem3, qsem4, sw, ssem, rsem,
                  px, p1, ps, p2, psem1, psem2, psem3, psem4, sa, ra, sb, rb):
     t = Pairs("gx", ngx)
@@ -252,12 +229,14 @@
     for i in range(min(slots, len(tiles))):
         fetch(i).start()
     swap = Swap("yz", nyz, sw, own, ssem, rsem)
-    greet(t.all() + swap.peers)
+    others = [{"gx": lax.rem(t.me + 1 + j, ngx)} for j in range(ngx - 1)]
+    greet(others + swap.peers)
+    normalize(Pairs("yz", nyz), others, s_ref, gain_ref, xg, stat, got, nss, nsr, nsa, nra, nsb, nrb)
 
     jobs = {}
 
-    def at(step, f):
-        jobs.setdefault(step, []).append(f)
+    def at(step, rank, f):
+        jobs.setdefault(step, []).append((rank, f))
 
     qred = Reduce(t, qx, q1, qs, q2, qsem1, qsem2, qsem3, qsem4)
     reds = [
@@ -281,17 +260,17 @@
         hid[t.me, :, c * w:(c + 1) * w] = (jax.nn.silu(both[:, :w]) * both[:, w:]).astype(BF)
         gats[c].start()
 
-    at(nq - 1, qred.start)
-    at(nq, qred.pass_on)
-    at(nq + 2, q_total)
+    at(nq - 1, 0, qred.start)
+    at(nq, 1, qred.pass_on)
+    at(nq + 3, 2, q_total)
     for c in range(nc):
         s = nq + 2 * c + 1
-        at(s, reds[c].start)
-        at(s + 1, reds[c].pass_on)
-        at(s + 3, lambda c=c: h_total(c))
-        at(s + 5, gats[c].pass_on)
-
-    x = x_ref[...]
+        at(s, 0, reds[c].start)
+        at(s + 1, 1, reds[c].pass_on)
+        at(s + 4, 2, lambda c=c: h_total(c))
+        at(s + 7, 3, gats[c].pass_on)
+
+    x = xg[...].reshape(ngx * r, xg.shape[2])
     for i in range(max(jobs) + 1):
         if i < len(tiles):
             fetch(i).wait()
@@ -304,8 +283,9 @@
             if i + slots < len(tiles):
                 fetch(i + slots).start()
             if i == nq - 1:
-                qx[:, :, qc:] = kv_ref[...].reshape(ngx, r, kv_ref.shape[1])
-        for f in jobs.get(i, []):
+                kv = jnp.dot(x, kvw[...], preferred_element_type=F32).astype(BF)
+                qx[:, :, qc:] = kv.reshape(ngx, r, kv.shape[1])
+        for _, f in sorted(jobs.get(i, []), key=lambda job: job[0]):
             f()
     for c in range(nc):
         reds[c].end()
@@ -314,8 +294,10 @@
     swap.end()
 
 
-def first(x, kv, qw, gw, uw, ngx, nyz):
-    batch, depth = x.shape
+def first(x, gain, kv, qw, gw, uw, ngx, nyz):
+    rows, depth = x.shape
+    batch, hy = rows * nyz, nyz // 2
+    gy = max(hy - 1, 1)
     qc, ff = qw.shape[1], gw.shape[1]
     w = 768 if qc % 768 == 0 and ff % 768 == 0 else 384
     nc = ff // w
@@ -323,7 +305,7 @@
     g = max(h - 1, 1)
     seqs = r // nyz
     width = qc + kv.shape[1]
-    slots = 4
+    slots = 9
     ANY = pl.BlockSpec(memory_space=pl.ANY)
     return pl.pallas_call(
         functools.partial(first_kernel, ngx, nyz, w),
@@ -331,9 +313,12 @@
             jax.ShapeDtypeStruct((ngx, r, ff), BF),
             jax.ShapeDtypeStruct((nyz, seqs, width), BF),
         ],
-        in_specs=[VM, VM, ANY, ANY, ANY],
+        in_specs=[VM, VM, VM, ANY, ANY, ANY],
         out_specs=[VM, VM],
         scratch_shapes=[
+            pltpu.VMEM((nyz, rows, depth), BF), pltpu.VMEM((2, rows, 128), F32),
+            pltpu.VMEM((ngx - 1, 2, rows, 128), F32), DMA((ngx - 1,)), DMA((ngx - 1,)),
+            DMA((gy,)), DMA((gy,)), DMA((hy,)), DMA((hy,)),
             pltpu.VMEM((slots, depth, w), BF), DMA((slots,)),
             pltpu.VMEM((ngx, r, width), BF), pltpu.VMEM((h, r, width), BF),
             pltpu.VMEM((g, r, width), BF), pltpu.VMEM((g, r, width), BF),
@@ -346,7 +331,7 @@
         ],
         compiler_params=params(1),
         name="project",
-    )(x, kv, qw, gw, uw)
+    )(x, gain.reshape(1, depth), kv, qw, gw, uw)
 
 
 def second_kernel(ngx, nyz, wd, wo, hid_ref, att_ref, dw, ow, out_ref,
@@ -377,7 +362,7 @@
         heads[tx.me] = jnp.concatenate([sw[i].astype(F32) for i in range(nyz)], axis=0).astype(BF)
         gat.start()
 
-    jobs = {2: join, 5: gat.pass_on}
+    jobs = {3: join, 7: gat.pass_on}
     hid = hid_ref[...]
     for i in range(nd):
         fetch(i).wait()
@@ -417,7 +402,7 @@
     no = cols // wo
     rx, r, hx, hy = batch // ngx, batch // nyz, ngx // 2, nyz // 2
     gx, gy = max(hx - 1, 1), max(hy - 1, 1)
-    slots = 4
+    slots = 9
     ANY = pl.BlockSpec(memory_space=pl.ANY)
     return pl.pallas_call(
         functools.partial(second_kernel, ngx, nyz, wd, wo),
@@ -477,15 +462,14 @@
 
 def body(ngx, nyz, stream, ln_gain, q_weight, kv_weight, out_weight, gate_weight, up_weight,
          down_weight, cache, lengths):
-    normed = norm_gather(stream, ln_gain, ngx, nyz)
-    batch = normed.shape[0]
+    batch = stream.shape[0] * nyz
     qc, kc = q_weight.shape[1], kv_weight.shape[1]
     pad = -(qc + kc) % 128
     seqs = batch // ngx // nyz
-
-    kv_part = jnp.dot(normed, kv_weight, preferred_element_type=F32).astype(BF)
-    kv_part = jnp.pad(kv_part, ((0, 0), (0, pad)))
-    hidden, qkv_own = first(normed, kv_part, q_weight, gate_weight, up_weight, ngx, nyz)
+    kv_padded = jnp.pad(kv_weight, ((0, 0), (0, pad)))
+    hidden, qkv_own = first(
+        stream, ln_gain, kv_padded, q_weight, gate_weight, up_weight, ngx, nyz
+    )
     qkv_own = jnp.swapaxes(qkv_own, 0, 1)
     query_own = qkv_own[:, :, :qc].reshape(seqs, nyz * qc)
     kv_own = qkv_own[:, :, qc:qc + kc].reshape(seqs, nyz * kc)

time: 98.6 us -> 87.5 us (0.89)
  Pallas kernels: 88.1 us -> 77 us
    pallas_call x1 -> x0, Pallas kernels: 20.5 us -> none  [norm_gather(): pl.pallas_call(functools.partial(norm_kernel, ngx, nyz), out_shape=jax.Sh...]
    pallas_call x1, Pallas kernels: 43.3 us -> 50.1 us  [first(): pl.pallas_call(functools.partial(first_kernel, ngx, nyz, w), out_shape=[j...]
    pallas_call x1, Pallas kernels: 24.4 us -> 26.9 us  [second(): pl.pallas_call(functools.partial(second_kernel, ngx, nyz, wd, wo), out_sh...]
where the time goes in v3:
time: 87.5 us; the launch traced here: 87.2 us
  Pallas kernels  77 us (88%)
  matrix products  5.77 us (7%)
  local copies, waits for them, and re-layouts  2.51 us (3%)
  other arithmetic  1.82 us (2%)
    pallas_call x1, Pallas kernels, first(): pl.pallas_call(functools.partial(first_kernel, ngx, nyz, w), out_shape=[j...  50.1 us
    pallas_call x1, Pallas kernels, second(): pl.pallas_call(functools.partial(second_kernel, ngx, nyz, wd, wo), out_sh...  26.9 us
    dot_general x1, matrix products, attend_local(): jnp.einsum('tgb,twb->tgw', query_vectors, key_rows, preferred_element_typ...  3.02 us
    dot_general x1, matrix products, attend_local(): jnp.einsum('aqc,acn->aqn', attention_probabilities, value_rows, preferred...  2.62 us

profile of v3, /device:TPU:0, one launch (start us, length us, event | category | flops | bytes accessed | tf_op | source)
XLA Modules:
  0.0 87.2 jit_solution(7582523737313153261)
XLA Ops:
  0.0 0.0 copy-start
  0.0 0.8 iota_compare_fusion
  0.8 0.7 reshape.35.gain_ref
  1.5 1.3 %copy.12 = bf16[2304,64]{1,0:T(8,128)(2,1)S(1)} copy(bf16[2304,64]{0,1:T(8,128)(2,1)} %param.13) | data formatting | bytes 589824 | tf_op args[3]
  2.7 0.1 pad.4.kvw
  2.9 0.0 copy-done
  2.9 50.1 %project.1 = (bf16[4,32,4608]{2,1,0:T(8,128)(2,1)S(1)}, bf16[8,4,1664]{2,1,0:T(4,128)(2,1)S(1)}) custom-call(bf16[16,2304]{1,0:T(8,128)(2,1)S(1)} %copy-done, bf16[1,2304]{1,0:T(2,128)(2,1)S(1)} %reshape.35.gain_ref, bf16[2304,128]{1,0:T(8,128)(2,1)S(1)} %pad.4.kvw, bf16[2304,1536]{1,0:T(8,128)(2,1)} %qw.1, bf16[2304,4608]{1,0:T(8,128)(2,1)} %gw.1, ...), custom_call_target="tpu_custom_call" | custom-call | tf_op jit(solution)/shard_map/project/pallas_call | solution.py:310
  53.1 0.1 reshape_reshape.6
  53.2 0.1 reshape.37
  53.3 0.1 fusion.18
  53.4 3.0 %select_reduce_fusion = (f32[4,48]{1,0:T(4,128)S(1)}, f32[4,48,1536]{2,1,0:T(8,128)S(1)}) fusion(f32[4,48]{1,0:T(4,128)S(1)} %broadcast_multiply_fusion, pred[4,1536]{1,0:T(4,128)(4,1)S(1)} %iota_compare_fusion, bf16[4,48,256]{2,1,0:T(8,128)(2,1)S(1)} %reshape_reshape.6, bf16[4,1536,512]{2,1,0:T(8,128)(2,1)} %param.18), kind=kOutput, calls=%fused_computation.7 | convolution fusion | flops 151879488 | bytes 4431360 | tf_op jit(solution)/shard_map/tgb,twb->tgw/dot_general | solution.py:438
  56.4 0.4 fusion.13
  56.8 2.6 %fusion.10 = bf16[4,48,256]{2,1,0:T(8,128)(2,1)S(1)} fusion(bf16[4,1536,512]{2,1,0:T(8,128)(2,1)} %param.18, f32[4,48,1536]{2,1,0:T(8,128)S(1)} %get-tuple-element.14, f32[4,48]{1,0:T(4,128)S(1)} %get-tuple-element.10, f32[4,48]{1,0:T(4,128)S(1)} %fusion.23, pred[4,1536]{1,0:T(4,128)(4,1)S(1)} %iota_compare_fusion, f32[4,256]{1,0:T(4,128)S(1)} %get-tuple-element.11, ...), kind=kOutput, calls=%fused_computation.9 | convolution fusion | flops 152322048 | bytes 4436224 | tf_op jit(solution)/shard_map/aqc,acn->aqn/dot_general | solution.py:453
  59.5 0.1 reshape_reshape.7
  59.6 0.1 copy.21
  59.6 26.9 %combine.1 = f32[16,2304]{1,0:T(8,128)S(1)} custom-call(bf16[128,4608]{1,0:T(8,128)(2,1)S(1)} %bitcast.11, bf16[8,4,1536]{2,1,0:T(4,128)(2,1)S(1)} %bitcast.12, bf16[4608,2304]{1,0:T(8,128)(2,1)} %dw.1, bf16[1536,2304]{1,0:T(8,128)(2,1)} %ow.1), custom_call_target="tpu_custom_call" | custom-call | tf_op jit(solution)/shard_map/combine/pallas_call | solution.py:407
  86.6 0.6 convert_element_type.25
  (8 shorter events, 0.1 us)
Async XLA Ops:
  0.0 2.9 %copy-start = (bf16[16,2304]{1,0:T(8,128)(2,1)S(1)}, bf16[16,2304]{1,0:T(8,128)(2,1)}, u32[]{:S(2)}) copy-start(bf16[16,2304]{1,0:T(8,128)(2,1)} %s_ref.1) | copy-start | bytes 221188
